TPU v7x, 32 devices: a whole 2x2x4 slice. The times are simulated.
32 devices in a mesh: grp: 4 (over z), tile: 8 (over y, x, core).
Axes of the slice: x: 2, y: 2, z: 4, core: 2. Of those that a mesh axis runs over, the one named last changes fastest.
Arguments:
- node_feats: bfloat16 [2048, 1024], P(('grp', 'tile')), may hold values from -6 to 6
- feature_table: bfloat16 [32768, 1024], P(('grp', 'tile')), may hold values from -6 to 6
- nbr_ids: int32 [2048, 8], P(('grp', 'tile')), may hold values from 0 to 32767, as said below
- degree: int32 [2048], P(('grp', 'tile')), may hold values from 1 to 8
- weight_in: bfloat16 [2048, 4096], P(None, 'tile'), may hold values from -0.125 to 0.125
- bias_in: float32 [4096], P('tile'), may hold values from -3 to 3
- weight_out: bfloat16 [4096, 1024], P('tile'), may hold values from -0.125 to 0.125
- bias_out: float32 [1024], replicated, may hold values from -3 to 3
Outputs:
- embedding: bfloat16 [2048, 1024], P(('grp', 'tile'))
Inputs may be any that keep to these rules, and one draw needn't show every extreme that they name: `nbr_ids`: table row r belongs to device r // 1024 in grp+tile order. Among the ids of the 64 nodes of one device, no owner device is named more than 32 times, and some owner exactly 32 times.
All inputs are finite; a program needn't handle non-finite values.
Results may differ from a plain program's by a relative error of at most 0.013.
Values may be sent and summed in bfloat16 or wider, within the bound.
A program may use at most 64 MiB of HBM per device.

v0:
```python
import jax
import jax.numpy as jnp
from jax import lax
from jax.sharding import PartitionSpec as P


def on_device(node_feats, feature_table, nbr_ids, degree, weight_in, bias_in, weight_out, bias_out):
    group_count = lax.axis_size("grp")
    tile_count = lax.axis_size("tile")
    nodes_here, nbr_count = nbr_ids.shape
    rows_here, feat_width = feature_table.shape
    ref_count = nodes_here * nbr_count
    devices = group_count * tile_count
    slot_cap = max(2, 2 * ref_count // devices)
    ref_ids = nbr_ids.reshape(ref_count)
    owner_dev = ref_ids // rows_here
    local_row = ref_ids - owner_dev * rows_here
    same_owner = owner_dev[:, None] == owner_dev[None, :]
    positions = jnp.arange(ref_count)
    earlier_ref = positions[:, None] < positions[None, :]
    ref_rank = jnp.sum((same_owner & earlier_ref).astype(jnp.int32), axis=0)
    ref_slot = owner_dev * slot_cap + ref_rank
    wanted = jnp.zeros((devices * slot_cap,), jnp.int32).at[ref_slot].set(local_row)
    wanted = wanted.reshape(group_count, tile_count, slot_cap)
    asked_rows = lax.all_to_all(
        lax.all_to_all(wanted, "grp", split_axis=0, concat_axis=0, tiled=True),
        "tile",
        split_axis=1,
        concat_axis=1,
        tiled=True,
    )
    found_rows = jnp.take(feature_table, asked_rows.reshape(-1), axis=0)
    found_rows = found_rows.reshape(group_count, tile_count, slot_cap, feat_width)
    came_rows = lax.all_to_all(
        lax.all_to_all(found_rows, "grp", split_axis=0, concat_axis=0, tiled=True),
        "tile",
        split_axis=1,
        concat_axis=1,
        tiled=True,
    )
    arrived = came_rows.reshape(devices * slot_cap, feat_width)
    chosen = jnp.take(arrived, ref_slot, axis=0).reshape(nodes_here, nbr_count, feat_width)
    live_mask = (jnp.arange(nbr_count)[None, :] < degree[:, None]).astype(jnp.bfloat16)
    summed = jnp.einsum("nk,nkd->nd", live_mask, chosen, preferred_element_type=jnp.float32)
    aggregate = (summed / degree.astype(jnp.float32)[:, None]).astype(jnp.bfloat16)
    joined = jnp.concatenate([node_feats, aggregate], axis=1)
    pre_act = jnp.dot(
        lax.all_gather(joined, "tile", axis=0, tiled=True),
        weight_in,
        preferred_element_type=jnp.float32,
    )
    hidden = jax.nn.relu(pre_act + bias_in).astype(jnp.bfloat16)
    summed_out = lax.psum_scatter(
        jnp.dot(hidden, weight_out, preferred_element_type=jnp.float32).astype(jnp.bfloat16),
        "tile",
        scatter_dimension=0,
        tiled=True,
    ).astype(jnp.float32)
    return (summed_out + bias_out).astype(jnp.bfloat16)


def solution(mesh):
    return jax.shard_map(
        on_device,
        mesh=mesh,
        in_specs=(
            P(("grp", "tile"), None),
            P(("grp", "tile"), None),
            P(("grp", "tile"), None),
            P(("grp", "tile")),
            P(None, "tile"),
            P("tile"),
            P("tile", None),
            P(),
        ),
        out_specs=P(("grp", "tile"), None),
        check_vma=False,
    )
```

profile of v0, /device:TPU:0, one launch (start us, length us, event | category | flops | bytes accessed | tf_op | source)
XLA Modules:
  0.0 207.9 jit_solution(4283456430751977614)
XLA Ops:
  6.5 0.0 copy-start
  6.5 0.9 copy.45
  7.5 0.1 reshape.199
  7.5 0.1 reshape.198
  7.7 0.2 convert_reduce_fusion
  7.9 2.4 %scatter_custom_fusion = s32[1024]{0:T(1024)S(1)} fusion(s32[512]{0:T(512)S(1)} %bitcast.29, s32[512]{0:T(512)S(1)} %get-tuple-element.5, s32[]{:T(128)} %constant.43.clone.1), kind=kCustom, calls=%fused_computation.51 | custom fusion | bytes 4100 | tf_op jit(solution)/shard_map/scatter | solution.py:23
  10.3 0.1 reshape.200
  10.4 0.1 reshape.231
  10.5 11.7 %all_to_all.20 = s32[4,1,256]{2,1,0:T(1,128)S(1)} all-to-all(s32[4,1,256]{2,1,0:T(1,128)S(1)} %reshape.231), channel_id=1, replica_groups=mesh['grp'=4,'tile'=8] {'grp'}, dimensions={0} | all-to-all | bytes 8192 | tf_op jit(solution)/shard_map/all_to_all | solution.py:26
  22.2 0.5 broadcast.211
  22.7 0.7 reduce
  23.4 0.1 reshape.232
  23.4 0.1 reshape.233
  23.5 8.2 %all_to_all.21 = s32[8,1,128]{2,1,0:T(1,128)S(1)} all-to-all(s32[8,1,128]{2,1,0:T(1,128)S(1)} %reshape.233), channel_id=1, replica_groups=mesh['grp'=4,'tile'=8] {'tile'}, dimensions={0} | all-to-all | bytes 8192 | tf_op jit(solution)/shard_map/all_to_all | solution.py:25
  31.7 0.7 reduce.1
  32.4 0.1 reshape.234
  32.5 0.1 reshape.201
  32.6 0.0 copy-done
  32.6 5.4 %gather_fusion = bf16[1024,1024]{1,0:T(8,128)(2,1)} fusion(bf16[1024,1024]{1,0:T(8,128)(2,1)S(1)} %copy-done, s32[1024]{0:T(1024)S(1)} %broadcast_clamp_fusion), kind=kCustom, calls=%fused_computation | custom fusion | bytes 4198400 | tf_op jit(solution)/shard_map/jit(_take)/gather | solution.py:32
  38.0 1.9 broadcast_select_fusion
  39.9 50.9 %all_to_all.22 = bf16[4,8,32,1024]{3,2,1,0:T(8,128)(2,1)S(1)} all-to-all(bf16[4,8,32,1024]{3,2,1,0:T(8,128)(2,1)S(1)} %broadcast_select_fusion), channel_id=1, replica_groups=mesh['grp'=4,'tile'=8] {'grp'}, dimensions={0} | all-to-all | bytes 4194304 | tf_op jit(solution)/shard_map/all_to_all | solution.py:35
  90.8 1.5 copy.54
  92.3 0.0 copy-start.3
  92.3 4.5 %all-to-all-start.3 = ((bf16[4,8,32,1024]{3,2,0,1:T(8,128)(2,1)}), bf16[4,8,32,1024]{3,2,0,1:T(8,128)(2,1)}, u32[]{:S(2)}, u32[]{:S(2)}) async-start(bf16[4,8,32,1024]{3,2,0,1:T(8,128)(2,1)} %copy.54), calls=%async_computation.3 | async-start | bytes 4194304 | tf_op jit(solution)/shard_map/all_to_all | solution.py:34
  96.8 0.0 all-gather.2.cloned.1.call-start
  96.8 0.1 reduce_sum.14
  96.9 0.0 copy-done.3
  96.9 0.1 fusion.13
  97.0 26.3 %all-to-all-done.3 = bf16[4,8,32,1024]{3,2,0,1:T(8,128)(2,1)} async-done(((bf16[4,8,32,1024]{3,2,0,1:T(8,128)(2,1)}), bf16[4,8,32,1024]{3,2,0,1:T(8,128)(2,1)}, u32[]{:S(2)}, u32[]{:S(2)}) %all-to-all-start.3) | async-done | bytes 2097184 | tf_op jit(solution)/shard_map/all_to_all | solution.py:34
  123.4 3.2 %copy.55 = bf16[4,8,32,1024]{3,2,1,0:T(8,128)(2,1)} copy(bf16[4,8,32,1024]{3,2,0,1:T(8,128)(2,1)} %all-to-all-done.3) | data formatting | bytes 4194304 | tf_op jit(solution)/shard_map/all_to_all | solution.py:34
  126.6 4.6 %gather_fusion.1 = bf16[512,1024]{1,0:T(8,128)(2,1)S(1)} fusion(bf16[1024,1024]{1,0:T(8,128)(2,1)} %bitcast.23, s32[1024]{0:T(1024)S(1)} %pad_clamp_fusion), kind=kCustom, calls=%fused_computation.1 | custom fusion | bytes 2099200 | tf_op jit(solution)/shard_map/jit(_take)/gather | solution.py:42
  131.1 0.0 copy-start.1
  131.2 0.0 copy-start.4
  131.2 0.5 fusion.2
  131.7 0.1 fusion.8
  131.8 0.3 copy-done.1
  132.1 0.8 pad_maximum_fusion
  132.8 0.0 all-gather.2.cloned.1.call-update
  132.8 0.0 copy-start.2
  132.8 0.0 reduce-scatter.2.cloned.1.call-start
  132.9 25.1 %all-gather.2.cloned.1.call-done = bf16[512,2048]{1,0:T(8,128)(2,1)} async-done(((bf16[64,2048]{1,0:T(8,128)(2,1)}), bf16[512,2048]{1,0:T(8,128)(2,1)}) %all-gather.2.cloned.1.call-update) | async-done | bytes 2097168 | tf_op jit(solution)/shard_map/all_gather | solution.py:48
  158.0 0.0 copy-done.4
  158.0 5.3 %convolution_convert_fusion = bf16[512,1024]{1,0:T(8,128)(2,1)} fusion(bf16[512,1024]{1,0:T(8,128)(2,1)} %param.14, bf16[512,2048]{1,0:T(8,128)(2,1)} %all-gather.2.cloned.1.call-done, bf16[2048,512]{1,0:T(8,128)(2,1)} %param.12, f32[512]{0:T(512)S(1)} %copy-done.4), kind=kOutput, calls=%fused_computation.4 | convolution fusion | flops 1611923456 | bytes 6293504 | tf_op jit(solution)/shard_map/dot_general | solution.py:54
  163.3 0.0 reduce-scatter.2.cloned.1.call-update
  163.3 36.1 %reduce-scatter.2.cloned.1.call-done = bf16[64,1024]{1,0:T(8,128)(2,1)} async-done(((bf16[512,1024]{1,0:T(8,128)(2,1)}), bf16[64,1024]{1,0:T(8,128)(2,1)}) %reduce-scatter.2.cloned.1.call-update) | async-done | bytes 131088 | tf_op jit(solution)/shard_map/reduce_scatter | solution.py:53
  199.4 0.0 copy-done.2
  199.4 1.6 add_convert_fusion
  (11 shorter events, 0.1 us)
Async XLA Ops:
  6.5 26.1 %copy-start = (bf16[1024,1024]{1,0:T(8,128)(2,1)S(1)}, bf16[1024,1024]{1,0:T(8,128)(2,1)}, u32[]{:S(2)}) copy-start(bf16[1024,1024]{1,0:T(8,128)(2,1)} %param.9) | copy-start | bytes 6291460
  92.3 4.6 %copy-start.3 = (s32[64]{0:T(128)S(1)}, s32[64]{0:T(128)}, u32[]{:S(2)}) copy-start(s32[64]{0:T(128)} %param.11) | copy-start | bytes 772
  92.3 31.1 %all-to-all-start.3 = ((bf16[4,8,32,1024]{3,2,0,1:T(8,128)(2,1)}), bf16[4,8,32,1024]{3,2,0,1:T(8,128)(2,1)}, u32[]{:S(2)}, u32[]{:S(2)}) async-start(bf16[4,8,32,1024]{3,2,0,1:T(8,128)(2,1)} %copy.54), calls=%async_computation.3 | async-start | bytes 4194304 | tf_op jit(solution)/shard_map/all_to_all | solution.py:34
  96.8 61.3 %all-gather.2.cloned.1.call-start = ((), (), s32[]{:S(2)}) async-start(), calls=%async_computation.5 | async-start | bytes 2359296 | tf_op jit(solution)/shard_map/all_gather | solution.py:48
  131.1 0.9 copy-start.1
  131.2 26.9 %copy-start.4 = (f32[512]{0:T(512)S(1)}, f32[512]{0:T(512)}, u32[]{:S(2)}) copy-start(f32[512]{0:T(512)} %param.13) | copy-start | bytes 6148
  132.8 66.6 %copy-start.2 = (f32[1024]{0:T(1024)S(1)}, f32[1024]{0:T(1024)}, u32[]{:S(2)}) copy-start(f32[1024]{0:T(1024)} %param.15) | copy-start | bytes 12292
  132.8 66.6 %reduce-scatter.2.cloned.1.call-start = ((), (), s32[]{:S(2)}) async-start(), calls=%async_computation.6 | async-start | bytes 1179648 | tf_op jit(solution)/shard_map/reduce_scatter | solution.py:53
Sparse Core Ops, SparseCore 0:
  133.0 25.0 all-gather.1
  163.4 35.9 reduce-scatter.1
where the time goes:
time: 208 us
  waiting for transfers between devices  87.6 us (42%)
  blocking collectives  70.8 us (34%)
  local copies, waits for them, and re-layouts  19.6 us (9%)
  between operations  13.6 us (7%)
  other arithmetic  5.97 us (3%)
  matrix products  5.78 us (3%)
  starting transfers between devices  4.55 us (2%)
    all_to_all x1, blocking collectives, on_device(): lax.all_to_all(found_rows, 'grp', split_axis=0, concat_axis=0, tiled=True)  50.9 us
    reduce_scatter x1, waiting for transfers between devices, on_device(): lax.psum_scatter(jnp.dot(hidden, weight_out, preferred_element_type=jnp.f...  36.1 us
    all_to_all x1, waiting for transfers between devices, on_device(): lax.all_to_all(lax.all_to_all(found_rows, 'grp', split_axis=0, concat_axi...  26.3 us
    all_gather x1, waiting for transfers between devices, on_device(): lax.all_gather(joined, 'tile', axis=0, tiled=True)  25.1 us
    all_to_all x1, blocking collectives, on_device(): lax.all_to_all(wanted, 'grp', split_axis=0, concat_axis=0, tiled=True)  11.7 us
    all_to_all x1, blocking collectives, on_device(): lax.all_to_all(lax.all_to_all(wanted, 'grp', split_axis=0, concat_axis=0,...  8.2 us
    gather x1, local copies, waits for them, and re-layouts, on_device(): found_rows = jnp.take(feature_table, asked_rows.reshape(-1), axis=0)  5.36 us
    dot_general x1, matrix products, on_device(): jnp.dot(hidden, weight_out, preferred_element_type=jnp.float32)  5.28 us
  transfers between devices with their start and end apart: 3, of which 3 were waited for; matrix products, arithmetic and copies ran while one was open for 0% of the time, Pallas kernels for 0%

commit v1 on v0

--- a/solution.py
+++ b/solution.py
@@ -1,10 +1,17 @@
+import functools
+
 import jax
 import jax.numpy as jnp
 from jax import lax
+from jax.experimental import pallas as pl
+from jax.experimental.pallas import tpu as pltpu
 from jax.sharding import PartitionSpec as P
 
-
-def on_device(node_feats, feature_table, nbr_ids, degree, weight_in, bias_in, weight_out, bias_out):
+MESH = pl.DeviceIdType.MESH
+LANES = 128
+
+
+def on_device_xla(node_feats, feature_table, nbr_ids, degree, weight_in, bias_in, weight_out, bias_out):
     group_count = lax.axis_size("grp")
     tile_count = lax.axis_size("tile")
     nodes_here, nbr_count = nbr_ids.shape
@@ -59,7 +66,317 @@
     return (summed_out + bias_out).astype(jnp.bfloat16)
 
 
+def layer_kernel(
+    groups,
+    ids_ref, deg_ref, feats_hbm, table_hbm, win_hbm, bin_ref, wout_hbm, bout_ref,
+    out_ref,
+    table, win, wout, feats_own, idbuf, keys, rowkeys, count,
+    sum_a, sum_b, rx, own_sum, zsend, zrecv, feats_all, agg_all, part, pouts, prx, qsend, qrx,
+    ldsem, tsem, idsem_s, idsem_r, rs_s, rs_r, z_s, z_r, fg_s, fg_r, ag_s, ag_r, pp_s, pp_r, q_s, q_r,
+):
+    f32, bf16 = jnp.float32, jnp.bfloat16
+    g = lax.axis_index("grp")
+    t = lax.axis_index("tile")
+    c = lax.rem(t, 2)
+    x = lax.rem(t // 2, 2)
+    y = t // 4
+    rows, width = table_hbm.shape
+    nodes = feats_hbm.shape[0]
+    half = width // 2
+    slots = ids_ref.shape[0]
+
+    def dev(dg, rel, dc=0):
+        xx = lax.rem(x + rel % 2, 2)
+        yy = lax.rem(y + rel // 2, 2)
+        cc = lax.rem(c + dc, 2)
+        return (lax.rem(g + dg, groups), (yy * 2 + xx) * 2 + cc)
+
+    def remote(src, dst, ss, rs, where):
+        return pltpu.make_async_remote_copy(
+            src_ref=src, dst_ref=dst, send_sem=ss, recv_sem=rs, device_id=where, device_id_type=MESH
+        )
+
+    mine = pl.ds(pl.multiple_of(c * rows, rows), rows)
+    loads = [
+        pltpu.make_async_copy(table_hbm, table.at[mine], ldsem.at[0]),
+        pltpu.make_async_copy(feats_hbm, feats_all.at[0, 0], ldsem.at[1]),
+        pltpu.make_async_copy(win_hbm, win, ldsem.at[2]),
+        pltpu.make_async_copy(wout_hbm, wout, ldsem.at[3]),
+        pltpu.make_async_copy(feats_hbm, feats_own, ldsem.at[4]),
+    ]
+    for load in loads:
+        load.start()
+
+    barrier = pltpu.get_barrier_semaphore()
+    peers = [dev(dg, rel) for dg in range(groups) for rel in range(4) if dg or rel]
+    peers.append(dev(0, 0, 1))
+    for where in peers:
+        pl.semaphore_signal(barrier, inc=1, device_id=where, device_id_type=MESH)
+
+    lane = lax.broadcasted_iota(jnp.int32, (16, 2 * rows), 1)
+    rowkeys[...] = jnp.left_shift(lax.rem(lane, LANES) + LANES, lane // LANES).astype(f32).astype(bf16)
+    idbuf[groups - 1, 0] = ids_ref[...]
+
+    pl.semaphore_wait(barrier, len(peers))
+
+    id_sends = []
+    for i in range(groups):
+        for rel in range(4):
+            if i == groups - 1 and rel == 0:
+                continue
+            send = remote(ids_ref, idbuf.at[i, rel], idsem_s.at[i, rel], idsem_r.at[i, rel],
+                          dev(groups - 1 - i, rel))
+            send.start()
+            id_sends.append(send)
+    tsend = remote(table_hbm, table.at[mine], tsem.at[0], tsem.at[1], dev(0, 0, 1))
+    tsend.start()
+    loads[4].wait()
+    fsends = []
+    for rel in (3, 1, 2):
+        send = remote(feats_own, feats_all.at[0, rel], fg_s.at[0, rel], fg_r.at[0, rel], dev(0, rel))
+        send.start()
+        fsends.append(send)
+    send = remote(feats_own, feats_all.at[1, 0], fg_s.at[1, 0], fg_r.at[1, 0], dev(0, 0, 1))
+    send.start()
+    fsends.append(send)
+
+    for send in id_sends:
+        send.wait_recv()
+    base = (g * lax.axis_size("tile") + (y * 2 + x) * 2) * rows
+    local = idbuf[...].reshape(groups * 4 * slots, LANES) - base
+    inside = (local >= 0) & (local < 2 * rows)
+    safe = jnp.where(inside, local, 0)
+    key = jnp.left_shift(lax.rem(safe, LANES) + LANES, safe // LANES)
+    keyf = jnp.where(inside, key, 0).astype(f32)
+    if keyf.shape[0] < LANES:
+        keyf = jnp.concatenate([keyf, jnp.zeros((LANES - keyf.shape[0], LANES), f32)], axis=0)
+    keys[...] = keyf.T
+
+    loads[0].wait()
+    tsend.wait_recv()
+
+    def rs_copy(kind, i):
+        src = (sum_a.at[i, 3], sum_a.at[i, 1], sum_b.at[i, 3], sum_b.at[i, 2],
+               sum_a.at[i, 2], sum_b.at[i, 1])[kind]
+        return remote(src, rx.at[kind, i], rs_s.at[kind, i], rs_r.at[kind, i],
+                      dev(0, (1, 1, 2, 2, 2, 1)[kind]))
+
+    one = jnp.ones((16, 2 * rows), bf16)
+    zero = jnp.zeros((16, 2 * rows), bf16)
+
+    def make_sums(i):
+        for rel in range(4):
+            block = i * 4 + rel
+
+            def group(r, carry, rel=rel, block=block):
+                at = pl.ds(pl.multiple_of(r * 16, 16), 16)
+                kk = keys[at, :]
+                rk = rowkeys[...]
+                total = zero
+                for k in range(slots):
+                    col = block * slots + k
+                    wide = jnp.broadcast_to(kk[:, col:col + 1], (16, LANES)).astype(bf16)
+                    wide = jnp.concatenate([wide] * (2 * rows // LANES), axis=1)
+                    total = total + jnp.where(wide == rk, one, zero)
+                count[pl.ds(pl.multiple_of(rel * nodes + r * 16, 16), 16), :] = total
+                return carry
+
+            lax.fori_loop(0, nodes // 16, group, 0)
+        step = min(256, half)
+        for n0 in range(0, width, step):
+            got = jnp.dot(count[...], table[:, n0:n0 + step], preferred_element_type=f32).astype(bf16)
+            into, at = (sum_a, n0) if n0 < half else (sum_b, n0 - half)
+            into[i, :, :, at:at + step] = got.reshape(4, nodes, step)
+        for kind in (0, 2, 1, 3):
+            rs_copy(kind, i).start()
+
+    def pass_on(i):
+        rs_copy(0, i).wait_recv()
+        sum_a[i, 2] = (sum_a[i, 2].astype(f32) + rx[0, i].astype(f32)).astype(bf16)
+        rs_copy(4, i).start()
+        rs_copy(2, i).wait_recv()
+        sum_b[i, 1] = (sum_b[i, 1].astype(f32) + rx[2, i].astype(f32)).astype(bf16)
+        rs_copy(5, i).start()
+
+    def z_copy(i):
+        return remote(zsend.at[i], zrecv.at[i], z_s.at[i], z_r.at[i], dev(i + 1, 0))
+
+    def plane_sum(i):
+        for kind in (1, 4, 3, 5):
+            rs_copy(kind, i).wait_recv()
+        a = sum_a[i, 0].astype(f32) + rx[1, i].astype(f32) + rx[4, i].astype(f32)
+        b = sum_b[i, 0].astype(f32) + rx[3, i].astype(f32) + rx[5, i].astype(f32)
+        if i < groups - 1:
+            zsend[i, :, 0:half] = a.astype(bf16)
+            zsend[i, :, half:width] = b.astype(bf16)
+            z_copy(i).start()
+        else:
+            own_sum[:, 0:half] = a
+            own_sum[:, half:width] = b
+
+    def gather_copy(buf, ss, rs, kind, rel):
+        if kind == 0:
+            return remote(buf.at[0, 0], buf.at[0, rel], ss.at[0, rel], rs.at[0, rel], dev(0, rel))
+        return remote(buf.at[0, rel], buf.at[1, rel], ss.at[1, rel], rs.at[1, rel], dev(0, 0, 1))
+
+    make_sums(0)
+    make_sums(1)
+    loads[1].wait()
+    for rel in (1, 2, 3):
+        gather_copy(feats_all, fg_s, fg_r, 0, rel).wait_recv()
+        gather_copy(feats_all, fg_s, fg_r, 1, rel).start()
+    pass_on(0)
+    for i in range(2, groups):
+        make_sums(i)
+        pass_on(i - 1)
+        plane_sum(i - 2)
+
+    loads[2].wait()
+    for rel in range(4):
+        gather_copy(feats_all, fg_s, fg_r, 1, rel).wait_recv()
+    hid = win.shape[1]
+
+    part[...] = jnp.dot(
+        feats_all[...].reshape(8 * nodes, width), win[0:width, :], preferred_element_type=f32
+    ).reshape(2, 4, nodes, hid) + bin_ref[...].reshape(1, 1, 1, hid)
+
+    plane_sum(groups - 2)
+    pass_on(groups - 1)
+    plane_sum(groups - 1)
+
+    total = own_sum[...]
+    for i in range(groups - 1):
+        z_copy(i).wait_recv()
+        total = total + zrecv[i].astype(f32)
+    agg_all[0, 0] = (total / deg_ref[...]).astype(bf16)
+    for rel in (3, 1, 2):
+        gather_copy(agg_all, ag_s, ag_r, 0, rel).start()
+    gather_copy(agg_all, ag_s, ag_r, 1, 0).start()
+    loads[3].wait()
+
+    def p_copy(rel):
+        return remote(pouts.at[1, rel], prx.at[rel], pp_s.at[rel], pp_r.at[rel], dev(0, 0, 1))
+
+    def q_copy(rel):
+        return remote(qsend.at[rel - 1], qrx.at[rel - 1], q_s.at[rel - 1], q_r.at[rel - 1], dev(0, rel))
+
+    for rel in (1, 2, 3):
+        gather_copy(agg_all, ag_s, ag_r, 0, rel).wait_recv()
+        gather_copy(agg_all, ag_s, ag_r, 1, rel).start()
+    for rel in range(4):
+        gather_copy(agg_all, ag_s, ag_r, 1, rel).wait_recv()
+        both = agg_all[:, rel].reshape(2 * nodes, width)
+        pre = jnp.dot(both, win[width:2 * width, :], preferred_element_type=f32)
+        pre = pre + part[:, rel].reshape(2 * nodes, hid)
+        hidden = jnp.maximum(pre, 0.0).astype(bf16)
+        got = jnp.dot(hidden, wout[...], preferred_element_type=f32).astype(bf16)
+        pouts[:, rel] = got.reshape(2, nodes, got.shape[1])
+        p_copy(rel).start()
+    for rel in (3, 1, 2):
+        p_copy(rel).wait_recv()
+        qsend[rel - 1] = (pouts[0, rel].astype(f32) + prx[rel].astype(f32)).astype(bf16)
+        q_copy(rel).start()
+    p_copy(0).wait_recv()
+    final = pouts[0, 0].astype(f32) + prx[0].astype(f32) + bout_ref[...]
+    for rel in (1, 2, 3):
+        q_copy(rel).wait_recv()
+        final = final + qrx[rel - 1].astype(f32)
+    out_ref[...] = final.astype(bf16)
+
+    for send in id_sends + fsends:
+        send.wait_send()
+    tsend.wait_send()
+    for rel in (1, 2, 3):
+        gather_copy(feats_all, fg_s, fg_r, 1, rel).wait_send()
+        gather_copy(agg_all, ag_s, ag_r, 0, rel).wait_send()
+        q_copy(rel).wait_send()
+    for rel in range(4):
+        gather_copy(agg_all, ag_s, ag_r, 1, rel).wait_send()
+        p_copy(rel).wait_send()
+    for i in range(groups):
+        for kind in range(6):
+            rs_copy(kind, i).wait_send()
+        if i < groups - 1:
+            z_copy(i).wait_send()
+
+
+def on_device_fused(groups, node_feats, feature_table, nbr_ids, degree, weight_in, bias_in, weight_out, bias_out):
+    nodes, slots = nbr_ids.shape
+    rows, width = feature_table.shape
+    hid = weight_in.shape[1]
+    outw = weight_out.shape[1]
+    bf16, f32 = jnp.bfloat16, jnp.float32
+    live = jnp.arange(slots, dtype=jnp.int32)[:, None] < degree[None, :]
+    ids = jnp.pad(jnp.where(live, nbr_ids.T, -1), ((0, 0), (0, LANES - nodes)), constant_values=-1)
+    vmem = pl.BlockSpec(memory_space=pltpu.VMEM)
+    hbm = pl.BlockSpec(memory_space=pl.ANY)
+    half = width // 2
+    dma = pltpu.SemaphoreType.DMA
+    return pl.pallas_call(
+        functools.partial(layer_kernel, groups),
+        out_shape=jax.ShapeDtypeStruct((nodes, outw), bf16),
+        in_specs=[vmem, vmem, hbm, hbm, hbm, vmem, hbm, vmem],
+        out_specs=vmem,
+        scratch_shapes=[
+            pltpu.VMEM((2 * rows, width), bf16),
+            pltpu.VMEM((2 * width, hid), bf16),
+            pltpu.VMEM((hid, outw), bf16),
+            pltpu.VMEM((nodes, width), bf16),
+            pltpu.VMEM((groups, 4, slots, LANES), jnp.int32),
+            pltpu.VMEM((LANES, LANES), f32),
+            pltpu.VMEM((16, 2 * rows), bf16),
+            pltpu.VMEM((4 * nodes, 2 * rows), bf16),
+            pltpu.VMEM((groups, 4, nodes, half), bf16),
+            pltpu.VMEM((groups, 4, nodes, half), bf16),
+            pltpu.VMEM((6, groups, nodes, half), bf16),
+            pltpu.VMEM((nodes, width), f32),
+            pltpu.VMEM((groups - 1, nodes, width), bf16),
+            pltpu.VMEM((groups - 1, nodes, width), bf16),
+            pltpu.VMEM((2, 4, nodes, width), bf16),
+            pltpu.VMEM((2, 4, nodes, width), bf16),
+            pltpu.VMEM((2, 4, nodes, hid), f32),
+            pltpu.VMEM((2, 4, nodes, outw), bf16),
+            pltpu.VMEM((4, nodes, outw), bf16),
+            pltpu.VMEM((3, nodes, outw), bf16),
+            pltpu.VMEM((3, nodes, outw), bf16),
+            dma((5,)), dma((2,)),
+            dma((groups, 4)), dma((groups, 4)),
+            dma((6, groups)), dma((6, groups)),
+            dma((groups - 1,)), dma((groups - 1,)),
+            dma((2, 4)), dma((2, 4)),
+            dma((2, 4)), dma((2, 4)),
+            dma((4,)), dma((4,)),
+            dma((3,)), dma((3,)),
+        ],
+        compiler_params=pltpu.CompilerParams(
+            collective_id=0, has_side_effects=True, vmem_limit_bytes=48 * 1024 * 1024
+        ),
+    )(
+        ids, degree.astype(f32)[:, None], node_feats, feature_table, weight_in,
+        bias_in[None, :], weight_out, bias_out[None, :],
+    )
+
+
 def solution(mesh):
+    groups, tiles = mesh.shape["grp"], mesh.shape["tile"]
+
+    def on_device(node_feats, feature_table, nbr_ids, degree, *weights):
+        nodes, slots = nbr_ids.shape
+        rows, width = feature_table.shape
+        fits = (
+            tiles == 8
+            and groups > 2
+            and groups * 4 * slots <= LANES
+            and nodes <= LANES
+            and nodes % 16 == 0
+            and rows % LANES == 0
+            and 2 * rows // LANES <= 16
+            and width % (4 * LANES) == 0
+        )
+        if fits:
+            return on_device_fused(groups, node_feats, feature_table, nbr_ids, degree, *weights)
+        return on_device_xla(node_feats, feature_table, nbr_ids, degree, *weights)
+
     return jax.shard_map(
         on_device,
         mesh=mesh,

time: 208 us -> 65.7 us (0.32)
  waiting for transfers between devices: 87.6 us -> 0 us
  blocking collectives: 70.8 us -> 0 us
  Pallas kernels: 0 us -> 56.6 us
  between operations: 13.6 us -> 0.02 us
  local copies, waits for them, and re-layouts: 19.6 us -> 7.44 us
  matrix products: 5.78 us -> 0 us
  other arithmetic: 5.97 us -> 1.35 us
  starting transfers between devices: 4.55 us -> 0 us
    all_to_all x3 -> x0, blocking collectives: 70.8 us -> none  [the longest x1 50.9 us: on_device(): lax.all_to_all(found_rows, 'grp', split_axis=0, concat_axis=0, tiled=True)]
    pallas_call x0 -> x1, Pallas kernels: none -> 56.6 us  [on_device_fused(): pl.pallas_call(functools.partial(layer_kernel, groups), out_shape=jax.Sha...]
    reduce_scatter x1 -> x0, waiting for transfers between devices: 36.1 us -> none  [on_device(): lax.psum_scatter(jnp.dot(hidden, weight_out, preferred_element_type=jnp.f...]
    all_to_all x1 -> x0, waiting for transfers between devices: 26.3 us -> none  [on_device(): lax.all_to_all(lax.all_to_all(found_rows, 'grp', split_axis=0, concat_axi...]
    all_gather x1 -> x0, waiting for transfers between devices: 25.1 us -> none  [on_device(): lax.all_gather(joined, 'tile', axis=0, tiled=True)]
    gather x2 -> x0, local copies, waits for them, and re-layouts: 9.95 us -> none  [the longest x1 5.36 us: on_device(): found_rows = jnp.take(feature_table, asked_rows.reshape(-1), axis=0)]
    unnamed x15 -> x13, local copies, waits for them, and re-layouts: 1.55 us -> 7.33 us
    dot_general x2 -> x0, matrix products: 5.78 us -> none  [the longest x1 5.28 us: on_device(): jnp.dot(hidden, weight_out, preferred_element_type=jnp.float32)]
  transfers between devices with their start and end apart: 3 -> 0, of which waited for: 3 -> 0; matrix products, arithmetic and copies ran while one was open for 0% -> 0% of each run, Pallas kernels for 0% -> 0%
where the time goes in v1:
time: 65.7 us; the launch traced here: 65.4 us
  Pallas kernels  56.6 us (86%)
  local copies, waits for them, and re-layouts  7.44 us (11%)
  other arithmetic  1.35 us (2%)
    pallas_call x1, Pallas kernels, on_device_fused(): pl.pallas_call(functools.partial(layer_kernel, groups), out_shape=jax.Sha...  56.6 us
    unnamed x13, local copies, waits for them, and re-layouts  7.33 us

profile of v1, /device:TPU:0, one launch (start us, length us, event | category | flops | bytes accessed | tf_op | source)
XLA Modules:
  0.0 65.4 jit_solution(14045770980984639149)
XLA Ops:
  0.0 0.7 %convert_bitcast_fusion = f32[64,1]{0,1:T(1,128)S(1)} fusion(s32[64]{0:T(128)} %param.11), kind=kLoop, calls=%fused_computation.2 | loop fusion | flops 64 | bytes 512 | tf_op jit(solution)/shard_map/broadcast_in_dim | solution.py:355
  0.7 0.7 %bitcast_select_fusion = s32[8,64]{1,0:T(8,128)S(1)} fusion(s32[64,8]{0,1:T(8,128)} %param.10, s32[64]{0:T(128)} %param.11), kind=kLoop, calls=%fused_computation | loop fusion | flops 1024 | bytes 4352 | tf_op jit(solution)/shard_map/jit(_where)/select_n | solution.py:310
  1.4 0.1 copy.9.deg_ref
  1.5 0.0 copy-start
  1.5 1.6 %copy-done = bf16[1024,1024]{1,0:T(8,128)(2,1)S(1)} copy-done((bf16[1024,1024]{1,0:T(8,128)(2,1)S(1)}, bf16[1024,1024]{1,0:T(8,128)(2,1)}, u32[]{:S(2)}) %copy-start) | copy-done | bytes 2097176
  3.0 0.0 copy-start.1
  3.0 1.6 %copy-done.1 = bf16[2048,512]{1,0:T(8,128)(2,1)S(1)} copy-done((bf16[2048,512]{1,0:T(8,128)(2,1)S(1)}, bf16[2048,512]{1,0:T(8,128)(2,1)}, u32[]{:S(2)}) %copy-start.1) | copy-done | bytes 2097176
  4.6 0.0 copy-start.2
  4.6 1.2 %copy-done.2 = bf16[512,1024]{1,0:T(8,128)(2,1)S(1)} copy-done((bf16[512,1024]{1,0:T(8,128)(2,1)S(1)}, bf16[512,1024]{1,0:T(8,128)(2,1)}, u32[]{:S(2)}) %copy-start.2) | copy-done | bytes 1048600
  5.9 0.0 copy-start.3
  5.9 0.9 %copy-done.3 = bf16[64,1024]{1,0:T(8,128)(2,1)S(1)} copy-done((bf16[64,1024]{1,0:T(8,128)(2,1)S(1)}, bf16[64,1024]{1,0:T(8,128)(2,1)}, u32[]{:S(2)}) %copy-start.3) | copy-done | bytes 131096
  6.8 0.0 copy-start.4
  6.8 0.7 %copy-done.4 = f32[1024]{0:T(1024)S(1)} copy-done((f32[1024]{0:T(1024)S(1)}, f32[1024]{0:T(1024)}, u32[]{:S(2)}) %copy-start.4) | copy-done | bytes 4120
  7.5 0.0 copy-start.5
  7.5 0.7 %copy-done.5 = f32[512]{0:T(512)S(1)} copy-done((f32[512]{0:T(512)S(1)}, f32[512]{0:T(512)}, u32[]{:S(2)}) %copy-start.5) | copy-done | bytes 2072
  8.1 56.6 %shard_map.82 = bf16[64,1024]{1,0:T(8,128)(2,1)S(1)} custom-call(s32[8,128]{1,0:T(8,128)S(1)} %pad.4.ids_ref, f32[64,1]{1,0:T(8,128)S(1)} %copy.9.deg_ref, bf16[64,1024]{1,0:T(8,128)(2,1)S(1)} %copy-done.3, bf16[1024,1024]{1,0:T(8,128)(2,1)S(1)} %copy-done, bf16[2048,512]{1,0:T(8,128)(2,1)S(1)} %copy-done.1, f32[1,512]{1,0:T(1,128)S(1)} %bitcast.7, ...), custom_call_target="tpu_custom_call" | custom-call | tf_op jit(solution)/shard_map/pallas_call | solution.py:315
  64.7 0.7 %copy.11 = bf16[64,1024]{1,0:T(8,128)(2,1)} copy(bf16[64,1024]{1,0:T(8,128)(2,1)S(1)} %shard_map.82) | data formatting | bytes 262144
  (1 shorter events, 0.0 us)
Async XLA Ops:
  1.5 1.6 %copy-start = (bf16[1024,1024]{1,0:T(8,128)(2,1)S(1)}, bf16[1024,1024]{1,0:T(8,128)(2,1)}, u32[]{:S(2)}) copy-start(bf16[1024,1024]{1,0:T(8,128)(2,1)} %table_hbm.1) | copy-start | bytes 6291460
  3.0 1.6 %copy-start.1 = (bf16[2048,512]{1,0:T(8,128)(2,1)S(1)}, bf16[2048,512]{1,0:T(8,128)(2,1)}, u32[]{:S(2)}) copy-start(bf16[2048,512]{1,0:T(8,128)(2,1)} %win_hbm.1) | copy-start | bytes 6291460
  4.6 1.2 %copy-start.2 = (bf16[512,1024]{1,0:T(8,128)(2,1)S(1)}, bf16[512,1024]{1,0:T(8,128)(2,1)}, u32[]{:S(2)}) copy-start(bf16[512,1024]{1,0:T(8,128)(2,1)} %wout_hbm.1) | copy-start | bytes 3145732
  5.9 0.9 %copy-start.3 = (bf16[64,1024]{1,0:T(8,128)(2,1)S(1)}, bf16[64,1024]{1,0:T(8,128)(2,1)}, u32[]{:S(2)}) copy-start(bf16[64,1024]{1,0:T(8,128)(2,1)} %feats_hbm.1) | copy-start | bytes 393220
  6.8 0.7 %copy-start.4 = (f32[1024]{0:T(1024)S(1)}, f32[1024]{0:T(1024)}, u32[]{:S(2)}) copy-start(f32[1024]{0:T(1024)} %param.15) | copy-start | bytes 12292
  7.5 0.7 %copy-start.5 = (f32[512]{0:T(512)S(1)}, f32[512]{0:T(512)}, u32[]{:S(2)}) copy-start(f32[512]{0:T(512)} %param.13) | copy-start | bytes 6148

commit v2 on v1

--- a/solution.py
+++ b/solution.py
@@ -68,8 +68,9 @@
 
 def layer_kernel(
     groups,
-    ids_ref, deg_ref, feats_hbm, table_hbm, win_hbm, bin_ref, wout_hbm, bout_ref,
+    ids_hbm, deg_hbm, feats_hbm, table_hbm, win_hbm, bin_hbm, wout_hbm, bout_hbm,
     out_ref,
+    ids_raw, deg_raw, bin_ref, bout_ref, ids_ref, deg_row, deg_col,
     table, win, wout, feats_own, idbuf, keys, rowkeys, count,
     sum_a, sum_b, rx, own_sum, zsend, zrecv, feats_all, agg_all, part, pouts, prx, qsend, qrx,
     ldsem, tsem, idsem_s, idsem_r, rs_s, rs_r, z_s, z_r, fg_s, fg_r, ag_s, ag_r, pp_s, pp_r, q_s, q_r,
@@ -83,7 +84,7 @@
     rows, width = table_hbm.shape
     nodes = feats_hbm.shape[0]
     half = width // 2
-    slots = ids_ref.shape[0]
+    slots = ids_hbm.shape[0]
 
     def dev(dg, rel, dc=0):
         xx = lax.rem(x + rel % 2, 2)
@@ -103,9 +104,13 @@
         pltpu.make_async_copy(win_hbm, win, ldsem.at[2]),
         pltpu.make_async_copy(wout_hbm, wout, ldsem.at[3]),
         pltpu.make_async_copy(feats_hbm, feats_own, ldsem.at[4]),
+        pltpu.make_async_copy(ids_hbm, ids_raw, ldsem.at[5]),
+        pltpu.make_async_copy(deg_hbm, deg_raw, ldsem.at[6]),
+        pltpu.make_async_copy(bin_hbm, bin_ref, ldsem.at[7]),
+        pltpu.make_async_copy(bout_hbm, bout_ref, ldsem.at[8]),
     ]
-    for load in loads:
-        load.start()
+    for at in (5, 6, 4, 0, 1, 2, 7, 3, 8):
+        loads[at].start()
 
     barrier = pltpu.get_barrier_semaphore()
     peers = [dev(dg, rel) for dg in range(groups) for rel in range(4) if dg or rel]
@@ -115,7 +120,16 @@
 
     lane = lax.broadcasted_iota(jnp.int32, (16, 2 * rows), 1)
     rowkeys[...] = jnp.left_shift(lax.rem(lane, LANES) + LANES, lane // LANES).astype(f32).astype(bf16)
+    loads[5].wait()
+    loads[6].wait()
+    degree = deg_raw[...]
+    live = lax.broadcasted_iota(jnp.int32, (slots, nodes), 0) < degree
+    if nodes < LANES:
+        ids_ref[...] = jnp.full((slots, LANES), -1, jnp.int32)
+    ids_ref[:, 0:nodes] = jnp.where(live, ids_raw[...], -1)
     idbuf[groups - 1, 0] = ids_ref[...]
+    deg_row[...] = jnp.ones((1, LANES), f32)
+    deg_row[:, 0:nodes] = degree.astype(f32)
 
     pl.semaphore_wait(barrier, len(peers))
 
@@ -140,6 +154,7 @@
     send.start()
     fsends.append(send)
 
+    deg_col[...] = jnp.broadcast_to(deg_row[...], (LANES, LANES)).T
     for send in id_sends:
         send.wait_recv()
     base = (g * lax.axis_size("tile") + (y * 2 + x) * 2) * rows
@@ -232,6 +247,7 @@
         plane_sum(i - 2)
 
     loads[2].wait()
+    loads[7].wait()
     for rel in range(4):
         gather_copy(feats_all, fg_s, fg_r, 1, rel).wait_recv()
     hid = win.shape[1]
@@ -248,11 +264,13 @@
     for i in range(groups - 1):
         z_copy(i).wait_recv()
         total = total + zrecv[i].astype(f32)
-    agg_all[0, 0] = (total / deg_ref[...]).astype(bf16)
+    divisor = jnp.concatenate([deg_col[0:nodes, :]] * (width // LANES), axis=1)
+    agg_all[0, 0] = (total / divisor).astype(bf16)
     for rel in (3, 1, 2):
         gather_copy(agg_all, ag_s, ag_r, 0, rel).start()
     gather_copy(agg_all, ag_s, ag_r, 1, 0).start()
     loads[3].wait()
+    loads[8].wait()
 
     def p_copy(rel):
         return remote(pouts.at[1, rel], prx.at[rel], pp_s.at[rel], pp_r.at[rel], dev(0, 0, 1))
@@ -260,10 +278,11 @@
     def q_copy(rel):
         return remote(qsend.at[rel - 1], qrx.at[rel - 1], q_s.at[rel - 1], q_r.at[rel - 1], dev(0, rel))
 
-    for rel in (1, 2, 3):
+    def forward(rel):
         gather_copy(agg_all, ag_s, ag_r, 0, rel).wait_recv()
         gather_copy(agg_all, ag_s, ag_r, 1, rel).start()
-    for rel in range(4):
+
+    def block(rel):
         gather_copy(agg_all, ag_s, ag_r, 1, rel).wait_recv()
         both = agg_all[:, rel].reshape(2 * nodes, width)
         pre = jnp.dot(both, win[width:2 * width, :], preferred_element_type=f32)
@@ -272,10 +291,22 @@
         got = jnp.dot(hidden, wout[...], preferred_element_type=f32).astype(bf16)
         pouts[:, rel] = got.reshape(2, nodes, got.shape[1])
         p_copy(rel).start()
-    for rel in (3, 1, 2):
+
+    def send_out(rel):
         p_copy(rel).wait_recv()
         qsend[rel - 1] = (pouts[0, rel].astype(f32) + prx[rel].astype(f32)).astype(bf16)
         q_copy(rel).start()
+
+    block(0)
+    forward(1)
+    forward(2)
+    block(1)
+    forward(3)
+    block(2)
+    send_out(1)
+    block(3)
+    send_out(2)
+    send_out(3)
     p_copy(0).wait_recv()
     final = pouts[0, 0].astype(f32) + prx[0].astype(f32) + bout_ref[...]
     for rel in (1, 2, 3):
@@ -306,18 +337,23 @@
     hid = weight_in.shape[1]
     outw = weight_out.shape[1]
     bf16, f32 = jnp.bfloat16, jnp.float32
-    live = jnp.arange(slots, dtype=jnp.int32)[:, None] < degree[None, :]
-    ids = jnp.pad(jnp.where(live, nbr_ids.T, -1), ((0, 0), (0, LANES - nodes)), constant_values=-1)
     vmem = pl.BlockSpec(memory_space=pltpu.VMEM)
-    hbm = pl.BlockSpec(memory_space=pl.ANY)
+    hbm = pl.BlockSpec(memory_space=pltpu.HBM)
     half = width // 2
     dma = pltpu.SemaphoreType.DMA
     return pl.pallas_call(
         functools.partial(layer_kernel, groups),
         out_shape=jax.ShapeDtypeStruct((nodes, outw), bf16),
-        in_specs=[vmem, vmem, hbm, hbm, hbm, vmem, hbm, vmem],
+        in_specs=[hbm] * 8,
         out_specs=vmem,
         scratch_shapes=[
+            pltpu.VMEM((slots, nodes), jnp.int32),
+            pltpu.VMEM((1, nodes), jnp.int32),
+            pltpu.VMEM((1, hid), f32),
+            pltpu.VMEM((1, outw), f32),
+            pltpu.VMEM((slots, LANES), jnp.int32),
+            pltpu.VMEM((1, LANES), f32),
+            pltpu.VMEM((LANES, LANES), f32),
             pltpu.VMEM((2 * rows, width), bf16),
             pltpu.VMEM((2 * width, hid), bf16),
             pltpu.VMEM((hid, outw), bf16),
@@ -339,7 +375,7 @@
             pltpu.VMEM((4, nodes, outw), bf16),
             pltpu.VMEM((3, nodes, outw), bf16),
             pltpu.VMEM((3, nodes, outw), bf16),
-            dma((5,)), dma((2,)),
+            dma((9,)), dma((2,)),
             dma((groups, 4)), dma((groups, 4)),
             dma((6, groups)), dma((6, groups)),
             dma((groups - 1,)), dma((groups - 1,)),
@@ -349,10 +385,10 @@
             dma((3,)), dma((3,)),
         ],
         compiler_params=pltpu.CompilerParams(
-            collective_id=0, has_side_effects=True, vmem_limit_bytes=48 * 1024 * 1024
+            collective_id=0, has_side_effects=True, vmem_limit_bytes=67043328
         ),
     )(
-        ids, degree.astype(f32)[:, None], node_feats, feature_table, weight_in,
+        nbr_ids.T, degree[None, :], node_feats, feature_table, weight_in,
         bias_in[None, :], weight_out, bias_out[None, :],
     )
 

time: 65.7 us -> 57.6 us (0.88)
  local copies, waits for them, and re-layouts: 7.44 us -> 1.57 us
  other arithmetic: 1.35 us -> 0 us
  Pallas kernels: 56.6 us -> 55.9 us
    unnamed x13 -> x1, local copies, waits for them, and re-layouts: 7.33 us -> 1.57 us
    select_n x1 -> x0, other arithmetic: 0.69 us -> none  [on_device_fused(): jnp.where(live, nbr_ids.T, -1)]
    pallas_call x1, Pallas kernels: 56.6 us -> 55.9 us  [on_device_fused(): pl.pallas_call(functools.partial(layer_kernel, groups), out_shape=jax.Sha...]
where the time goes in v2:
time: 57.6 us; the launch traced here: 57.5 us
  Pallas kernels  55.9 us (97%)
  local copies, waits for them, and re-layouts  1.57 us (3%)
    pallas_call x1, Pallas kernels, on_device_fused(): pl.pallas_call(functools.partial(layer_kernel, groups), out_shape=jax.Sha...  55.9 us
    unnamed x1, local copies, waits for them, and re-layouts  1.57 us

profile of v2, /device:TPU:0, one launch (start us, length us, event | category | flops | bytes accessed | tf_op | source)
XLA Modules:
  0.0 57.5 jit_solution(9954785136777056477)
XLA Ops:
  0.0 55.9 %shard_map.82 = bf16[64,1024]{1,0:T(8,128)(2,1)} custom-call(s32[8,64]{1,0:T(8,128)} %bitcast.4, s32[1,64]{1,0:T(1,128)} %bitcast.7, bf16[64,1024]{1,0:T(8,128)(2,1)} %feats_hbm.1, bf16[1024,1024]{1,0:T(8,128)(2,1)} %table_hbm.1, bf16[2048,512]{1,0:T(8,128)(2,1)} %win_hbm.1, f32[1,512]{1,0:T(1,128)} %bitcast.6, bf16[512,1024]{1,0:T(8,128)(2,1)} %wout_hbm.1, ...), custom_call_target="tpu_custom_call" | custom-call | tf_op jit(solution)/shard_map/pallas_call | solution.py:344
  55.9 1.6 %copy.10 = bf16[64,1024]{1,0:T(8,128)(2,1)} copy(bf16[64,1024]{1,0:T(8,128)(2,1)} %shard_map.82) | data formatting | bytes 262144

commit v3 on v2

--- a/solution.py
+++ b/solution.py
@@ -202,8 +202,11 @@
             got = jnp.dot(count[...], table[:, n0:n0 + step], preferred_element_type=f32).astype(bf16)
             into, at = (sum_a, n0) if n0 < half else (sum_b, n0 - half)
             into[i, :, :, at:at + step] = got.reshape(4, nodes, step)
-        for kind in (0, 2, 1, 3):
-            rs_copy(kind, i).start()
+            if n0 + step == half:
+                rs_copy(0, i).start()
+                rs_copy(1, i).start()
+        rs_copy(2, i).start()
+        rs_copy(3, i).start()
 
     def pass_on(i):
         rs_copy(0, i).wait_recv()
@@ -266,7 +269,7 @@
         total = total + zrecv[i].astype(f32)
     divisor = jnp.concatenate([deg_col[0:nodes, :]] * (width // LANES), axis=1)
     agg_all[0, 0] = (total / divisor).astype(bf16)
-    for rel in (3, 1, 2):
+    for rel in (1, 2, 3):
         gather_copy(agg_all, ag_s, ag_r, 0, rel).start()
     gather_copy(agg_all, ag_s, ag_r, 1, 0).start()
     loads[3].wait()

time: 57.6 us -> 57.9 us (level)
  no operation moved by 1% of the time
where the time goes in v3:
time: 57.9 us; the launch traced here: 57.7 us
  Pallas kernels  56.2 us (97%)
  local copies, waits for them, and re-layouts  1.57 us (3%)
    pallas_call x1, Pallas kernels, on_device_fused(): pl.pallas_call(functools.partial(layer_kernel, groups), out_shape=jax.Sha...  56.2 us
    unnamed x1, local copies, waits for them, and re-layouts  1.57 us

profile of v3, /device:TPU:0, one launch (start us, length us, event | category | flops | bytes accessed | tf_op | source)
XLA Modules:
  0.0 57.7 jit_solution(13321062401132991559)
XLA Ops:
  0.0 56.2 %shard_map.82 = bf16[64,1024]{1,0:T(8,128)(2,1)} custom-call(s32[8,64]{1,0:T(8,128)} %bitcast.4, s32[1,64]{1,0:T(1,128)} %bitcast.7, bf16[64,1024]{1,0:T(8,128)(2,1)} %feats_hbm.1, bf16[1024,1024]{1,0:T(8,128)(2,1)} %table_hbm.1, bf16[2048,512]{1,0:T(8,128)(2,1)} %win_hbm.1, f32[1,512]{1,0:T(1,128)} %bitcast.6, bf16[512,1024]{1,0:T(8,128)(2,1)} %wout_hbm.1, ...), custom_call_target="tpu_custom_call" | custom-call | tf_op jit(solution)/shard_map/pallas_call | solution.py:347
  56.2 1.6 %copy.10 = bf16[64,1024]{1,0:T(8,128)(2,1)} copy(bf16[64,1024]{1,0:T(8,128)(2,1)} %shard_map.82) | data formatting | bytes 262144
